TPU v7x, 32 devices: a whole 2x2x4 slice. The times are simulated.
32 devices in a mesh: groups: 2 (over y), dp: 4 (over z), layer: 4 (over x, core).
Axes of the slice: x: 2, y: 2, z: 4, core: 2. Of those that a mesh axis runs over, the one named last changes fastest.
Arguments:
- layer_inputs: float32 [4, 1024, 512], P('layer', ('groups', 'dp')), parts along dimension 1, may hold values from -6 to 6
- pre_acts: float32 [4, 1024, 512], P('layer', ('groups', 'dp')), parts along dimension 1, may hold values from -6 to 6
- layer_outputs: float32 [4, 1024, 512], P('layer', ('groups', 'dp')), parts along dimension 1, may hold values from -6 to 6
- multipliers: float32 [4, 1024, 512], P('layer', ('groups', 'dp')), parts along dimension 1, may hold values from -6 to 6
- weights: float32 [8, 512, 512], P(('groups', 'layer')), parts along dimension 0, may hold values from -0.25 to 0.25
- biases: float32 [8, 512], P(('groups', 'layer')), parts along dimension 0, may hold values from -3 to 3
- prev_outputs: float32 [1024, 512], P(('groups', 'dp')), parts along dimension 0, may hold values from -6 to 6
- prev_multipliers: float32 [1024, 512], P(('groups', 'dp')), parts along dimension 0, may hold values from -6 to 6
- next_inputs: float32 [1024, 512], P(('groups', 'dp')), parts along dimension 0, may hold values from -6 to 6
- row_order: int32 [8, 128], P(('groups', 'dp')), parts along dimension 0, may hold values from 0 to 127, each once within a row
Outputs:
- new_inputs: float32 [4, 1024, 512], P('layer', ('groups', 'dp')), parts along dimension 1
- new_preacts: float32 [4, 1024, 512], P('layer', ('groups', 'dp')), parts along dimension 1
- new_outputs: float32 [4, 1024, 512], P('layer', ('groups', 'dp')), parts along dimension 1
- new_multipliers: float32 [4, 1024, 512], P('layer', ('groups', 'dp')), parts along dimension 1
- new_weights: float32 [8, 512, 512], P(('groups', 'layer')), parts along dimension 0
- new_biases: float32 [8, 512], P(('groups', 'layer')), parts along dimension 0
There are 2 independent parts, one for each index of `groups`. A program takes and returns all parts, laid end to end along the dimension named above; each array names one. Nothing has to cross between parts.
Inputs may be any that keep to these rules, and one draw needn't show every extreme that they name: Each row of row_order holds every number of 0 to 127 once.
All inputs are finite; a program needn't handle non-finite values.
Results may differ from a plain program's by a relative error of at most 0.0001.
Values sent between devices are 32-bit elements; how exact they have to be, the bound alone decides.
A program may use at most 64 MiB of HBM per device.

v0:
```python
import jax
import jax.numpy as jnp
from jax import lax
from jax.sharding import PartitionSpec as P

INNER = 3


penalty_nu = 1.0
penalty_rho = 1.0
step_input = 0.2
step_weight = 0.3
step_preact = 0.5


def from_behind(x, axis, by):
    count = lax.axis_size(axis)
    pairs = [(i, i + by) for i in range(count) if 0 <= i + by < count]
    return lax.ppermute(x, axis, pairs)


def matmul(left, right):
    return jnp.dot(left, right, precision=lax.Precision.HIGHEST)


def body(
    layer_inputs,
    pre_acts,
    layer_outputs,
    multipliers,
    weights,
    biases,
    prev_outputs,
    prev_multipliers,
    next_inputs,
    row_order,
):
    row_perm = row_order[0]
    edge_outputs = jnp.take(prev_outputs, row_perm, axis=0)
    edge_duals = jnp.take(prev_multipliers, row_perm, axis=0)
    edge_inputs = jnp.take(next_inputs, row_perm, axis=0)
    first_layer = lax.axis_index("layer") == 0
    last_layer = lax.axis_index("layer") == lax.axis_size("layer") - 1
    row_count = layer_inputs.shape[1] * lax.axis_size("dp")
    scale = step_weight / row_count
    inputs, preact, outputs, duals = (
        layer_inputs[0],
        pre_acts[0],
        layer_outputs[0],
        multipliers[0],
    )
    weight, offset = (weights[0], biases[0])
    before_out, before_dual = from_behind((outputs, duals), "layer", 1)
    before_out = jnp.where(first_layer, edge_outputs, before_out)
    before_dual = jnp.where(first_layer, edge_duals, before_dual)
    coupling = before_dual + penalty_rho * (inputs - before_out)
    residual = matmul(inputs, weight) + offset[None, :] - preact
    inputs = inputs - step_input * (penalty_nu * matmul(residual, weight.T) + coupling)
    gram_matrix, cross_term, column_sums, preact_sums = lax.psum(
        (
            matmul(inputs.T, inputs),
            matmul(inputs.T, preact),
            jnp.sum(inputs, axis=0),
            jnp.sum(preact, axis=0),
        ),
        "dp",
    )
    for inner_step in range(INNER):
        grad_weight = (
            matmul(gram_matrix, weight) + column_sums[:, None] * offset[None, :] - cross_term
        )
        grad_offset = matmul(column_sums[None, :], weight)[0] + row_count * offset - preact_sums
        weight = weight - scale * grad_weight
        offset = offset - scale * grad_offset
    target = matmul(inputs, weight) + offset[None, :]
    preact = preact - step_preact * (
        preact - target + (jax.nn.softplus(preact) - outputs) * jax.nn.sigmoid(preact)
    )
    after_in = from_behind(inputs, "layer", -1)
    after_in = jnp.where(last_layer, edge_inputs, after_in)
    outputs = (penalty_nu * jax.nn.softplus(preact) + duals + penalty_rho * after_in) / (
        penalty_nu + penalty_rho
    )
    duals = duals + penalty_rho * (after_in - outputs)
    return (inputs[None], preact[None], outputs[None], duals[None], weight[None], offset[None])


def solution(mesh):
    return jax.shard_map(
        body,
        mesh=mesh,
        in_specs=(
            P("layer", ("groups", "dp"), None),
            P("layer", ("groups", "dp"), None),
            P("layer", ("groups", "dp"), None),
            P("layer", ("groups", "dp"), None),
            P(("groups", "layer"), None, None),
            P(("groups", "layer"), None),
            P(("groups", "dp"), None),
            P(("groups", "dp"), None),
            P(("groups", "dp"), None),
            P(("groups", "dp"), None),
        ),
        out_specs=(
            P("layer", ("groups", "dp"), None),
            P("layer", ("groups", "dp"), None),
            P("layer", ("groups", "dp"), None),
            P("layer", ("groups", "dp"), None),
            P(("groups", "layer"), None, None),
            P(("groups", "layer"), None),
        ),
        check_vma=False,
    )
```

profile of v0, /device:TPU:0, one launch (start us, length us, event | category | flops | bytes accessed | tf_op | source)
XLA Modules:
  0.0 131.0 jit_solution(5230148431243877205)
XLA Ops:
  7.2 0.0 copy-start
  7.2 0.0 all-reduce.4.cloned.1.call-start
  7.2 2.5 %collective-permute-start = (f32[128,512]{1,0:T(8,128)}, f32[128,512]{1,0:T(8,128)S(1)}, u32[]{:S(2)}, u32[]{:S(2)}) collective-permute-start(f32[128,512]{1,0:T(8,128)} %bitcast.95), channel_id=1, source_target_pairs={{0,1},{1,2},{2,3},{4,5},{5,6},{6,7},{8,9},{9,10},{10,11},{12,13},{... | collective-permute-start | bytes 786440 | tf_op jit(solution)/shard_map/ppermute | solution.py:19
  9.8 4.5 %collective-permute-start.1 = (f32[128,512]{1,0:T(8,128)}, f32[128,512]{1,0:T(8,128)S(1)}, u32[]{:S(2)}, u32[]{:S(2)}) collective-permute-start(f32[128,512]{1,0:T(8,128)} %bitcast.107), channel_id=1, source_target_pairs={{0,1},{1,2},{2,3},{4,5},{5,6},{6,7},{8,9},{9,10},{10,11},{12,13},{... | collective-permute-start | bytes 786440 | tf_op jit(solution)/shard_map/ppermute | solution.py:19
  14.4 0.8 gather_fusion
  15.1 0.2 copy-done.2
  15.3 0.8 gather_fusion.1
  16.1 0.4 copy-done.1
  16.5 0.0 copy-done.7
  16.6 0.1 copy-done.9
  16.7 0.2 copy-done.12
  16.9 0.7 fusion.13
  17.6 1.2 fusion.39
  18.8 2.0 %fusion.25 = f32[512,512]{1,0:T(8,128)} fusion(f32[128,512]{1,0:T(8,128)S(1)} %get-tuple-element.14, f32[1,128,512]{2,1,0:T(8,128)S(1)} %copy-done.7), kind=kOutput, calls=%fused_computation.38 | convolution fusion | flops 402653184 | bytes 1572864 | tf_op jit(solution)/shard_map/dot_general | solution.py:23
  20.8 2.0 %fusion.40 = f32[512,512]{1,0:T(8,128)} fusion(f32[128,512]{1,0:T(8,128)S(1)} %get-tuple-element.14), kind=kOutput, calls=%fused_computation.65 | convolution fusion | flops 402653184 | bytes 1310720 | tf_op jit(solution)/shard_map/dot_general | solution.py:23
  22.8 0.0 all-reduce.4.cloned.1.call-update
  22.9 0.9 copy-done.3
  23.8 0.8 gather_fusion.2
  24.6 1.3 collective-permute-start.2
  25.9 12.6 %all-reduce = (f32[512]{0:T(512)S(1)}, f32[512]{0:T(512)S(1)}) all-reduce(f32[512]{0:T(512)S(1)} %get-tuple-element.13, f32[512]{0:T(512)S(1)} %reduce_sum.19), channel_id=1, replica_groups=mesh['groups'=2,'dp'=4,'layer'=4] {'dp'}, use_global_device_ids=true, to_apply=%region_2.4 | all-reduce | flops 1024 | bytes 8192 | tf_op jit(solution)/shard_map/psum | solution.py:59
  38.5 0.6 fusion.15
  39.1 73.5 %all-reduce.4.cloned.1.call-done = (f32[512,512]{1,0:T(8,128)}, f32[512,512]{1,0:T(8,128)}) async-done(((f32[512,512]{1,0:T(8,128)}, f32[512,512]{1,0:T(8,128)}), (f32[512,512]{1,0:T(8,128)}, f32[512,512]{1,0:T(8,128)})) %all-reduce.4.cloned.1.call-update) | async-done | bytes 2097168 | tf_op jit(solution)/shard_map/psum | solution.py:59
  112.6 3.6 %fusion.4 = f32[512,512]{1,0:T(8,128)S(1)} fusion(f32[512,512]{1,0:T(8,128)} %get-tuple-element.9, f32[512,512]{1,0:T(8,128)} %get-tuple-element.10, f32[1,512,512]{2,1,0:T(8,128)S(1)} %copy-done.1, f32[512]{0:T(512)S(1)} %bitcast.102, f32[512]{0:T(512)S(1)} %get-tuple-element.7), kind=kOutput, calls=%fused_computation.10 | convolution fusion | flops 1611923456 | bytes 4198400 | tf_op jit(solution)/shard_map/dot_general | solution.py:23
  116.2 0.6 fusion.41
  116.8 0.6 copy-done.4
  117.4 2.0 %fusion.6 = f32[512,512]{1,0:T(8,128)S(1)} fusion(f32[512,512]{1,0:T(8,128)S(1)} %fusion.4, f32[512,512]{1,0:T(8,128)S(1)} %copy-done.4, f32[512,512]{1,0:T(8,128)S(1)} %copy-done.5, f32[512]{0:T(512)S(1)} %multiply_subtract_fusion.2, f32[512]{0:T(512)S(1)} %get-tuple-element.7), kind=kOutput, calls=%fused_computation.12 | convolution fusion | flops 1611923456 | bytes 4198400 | tf_op jit(solution)/shard_map/dot_general | solution.py:23
  119.3 0.6 fusion.42
  120.0 2.0 %fusion.8 = f32[512,512]{1,0:T(8,128)S(1)} fusion(f32[512,512]{1,0:T(8,128)S(1)} %fusion.6, f32[512,512]{1,0:T(8,128)S(1)} %copy-done.4, f32[512,512]{1,0:T(8,128)S(1)} %copy-done.5, f32[512]{0:T(512)S(1)} %get-tuple-element.12, f32[512]{0:T(512)S(1)} %get-tuple-element.7), kind=kOutput, calls=%fused_computation.14 | convolution fusion | flops 1611923456 | bytes 4198400 | tf_op jit(solution)/shard_map/dot_general | solution.py:23
  122.0 0.9 fusion.12
  122.9 0.0 copy-done.8
  122.9 0.2 copy-done.10
  123.2 1.0 add_bitcast_fusion
  (31 shorter events, 0.1 us)
Async XLA Ops:
  7.2 7.2 %copy-start = (f32[128,512]{1,0:T(8,128)S(1)}, f32[128,512]{1,0:T(8,128)}, u32[]{:S(2)}) copy-start(f32[128,512]{1,0:T(8,128)} %param.19) | copy-start | bytes 786436
  7.2 105.4 %all-reduce.4.cloned.1.call-start = ((), (), s32[]{:S(2)}) async-start(), calls=%async_computation | async-start | bytes 4194304 | tf_op jit(solution)/shard_map/psum | solution.py:59
  7.2 10.4 %collective-permute-start = (f32[128,512]{1,0:T(8,128)}, f32[128,512]{1,0:T(8,128)S(1)}, u32[]{:S(2)}, u32[]{:S(2)}) collective-permute-start(f32[128,512]{1,0:T(8,128)} %bitcast.95), channel_id=1, source_target_pairs={{0,1},{1,2},{2,3},{4,5},{5,6},{6,7},{8,9},{9,10},{10,11},{12,13},{... | collective-permute-start | bytes 786440 | tf_op jit(solution)/shard_map/ppermute | solution.py:19
  9.8 4.5 %copy-start.15 = (s32[1,128]{1,0:T(1,128)S(1)}, s32[1,128]{1,0:T(1,128)}, u32[]{:S(2)}) copy-start(s32[1,128]{1,0:T(1,128)} %param.21) | copy-start | bytes 1540
  9.8 7.8 %collective-permute-start.1 = (f32[128,512]{1,0:T(8,128)}, f32[128,512]{1,0:T(8,128)S(1)}, u32[]{:S(2)}, u32[]{:S(2)}) collective-permute-start(f32[128,512]{1,0:T(8,128)} %bitcast.107), channel_id=1, source_target_pairs={{0,1},{1,2},{2,3},{4,5},{5,6},{6,7},{8,9},{9,10},{10,11},{12,13},{... | collective-permute-start | bytes 786440 | tf_op jit(solution)/shard_map/ppermute | solution.py:19
  14.4 1.0 copy-start.2
  15.3 1.2 copy-start.1
  15.3 1.3 copy-start.7
  15.3 1.3 %copy-start.9 = (f32[1,128,512]{2,1,0:T(8,128)S(1)}, f32[1,128,512]{2,1,0:T(8,128)}, u32[]{:S(2)}) copy-start(f32[1,128,512]{2,1,0:T(8,128)} %param.12) | copy-start | bytes 786436
  16.1 0.8 copy-start.12
  18.8 103.2 %copy-start.6 = (f32[128,512]{1,0:T(8,128)}, f32[128,512]{1,0:T(8,128)S(1)}, u32[]{:S(2)}) copy-start(f32[128,512]{1,0:T(8,128)S(1)} %get-tuple-element.14) | copy-start | bytes 786436
  22.9 1.0 copy-start.3
  24.6 98.4 %collective-permute-start.2 = (f32[128,512]{1,0:T(8,128)S(1)}, f32[128,512]{1,0:T(8,128)S(1)}, u32[]{:S(2)}, u32[]{:S(2)}) collective-permute-start(f32[128,512]{1,0:T(8,128)S(1)} %get-tuple-element.14), channel_id=1, source_target_pairs={{1,0},{2,1},{3,2},{5,4},{6,5},{7,6},{9,8},{10,9},{11,10},{13,12},{... | collective-permute-start | bytes 786440 | tf_op jit(solution)/shard_map/ppermute | solution.py:19
  112.6 4.2 %copy-start.5 = (f32[512,512]{1,0:T(8,128)S(1)}, f32[512,512]{1,0:T(8,128)}, u32[]{:S(2)}) copy-start(f32[512,512]{1,0:T(8,128)} %get-tuple-element.10) | copy-start | bytes 3145732
  116.1 1.2 copy-start.4
  120.0 2.0 %copy-start.13 = (f32[512]{0:T(512)}, f32[512]{0:T(512)S(1)}, u32[]{:S(2)}) copy-start(f32[512]{0:T(512)S(1)} %get-tuple-element.11) | copy-start | bytes 6148
  120.0 2.0 %copy-start.14 = (f32[1,128,512]{2,1,0:T(8,128)S(1)}, f32[1,128,512]{2,1,0:T(8,128)}, u32[]{:S(2)}) copy-start(f32[1,128,512]{2,1,0:T(8,128)} %param.14) | copy-start | bytes 786436
  122.0 1.0 copy-start.8
  122.0 1.1 copy-start.10
  122.9 1.2 copy-start.11
Sparse Core Ops, SparseCore 0:
  23.0 89.5 all-reduce.3
where the time goes:
time: 131 us
  waiting for transfers between devices  73.5 us (56%)
  matrix products  16.1 us (12%)
  between operations  14.3 us (11%)
  blocking collectives  12.6 us (10%)
  starting transfers between devices  8.38 us (6%)
  local copies, waits for them, and re-layouts  5.07 us (4%)
    psum x1, waiting for transfers between devices, body(): lax.psum((matmul(inputs.T, inputs), matmul(inputs.T, preact), jnp.sum(inp...  73.5 us
    dot_general x11, matrix products, matmul(): return jnp.dot(left, right, precision=lax.Precision.HIGHEST)  16.1 us
    psum x1, blocking collectives, body(): lax.psum((matmul(inputs.T, inputs), matmul(inputs.T, preact), jnp.sum(inp...  12.6 us
    ppermute x3, starting transfers between devices, from_behind(): return lax.ppermute(x, axis, pairs)  8.34 us
    unnamed x32, local copies, waits for them, and re-layouts  2.81 us
  transfers between devices with their start and end apart: 4, of which 1 were waited for; matrix products, arithmetic and copies ran while one was open for 10% of the time, Pallas kernels for 0%

commit v1 on v0

--- a/solution.py
+++ b/solution.py
@@ -1,6 +1,10 @@
+import functools
+
 import jax
 import jax.numpy as jnp
 from jax import lax
+from jax.experimental import pallas as pl
+from jax.experimental.pallas import tpu as pltpu
 from jax.sharding import PartitionSpec as P
 
 INNER = 3
@@ -23,7 +27,7 @@
     return jnp.dot(left, right, precision=lax.Precision.HIGHEST)
 
 
-def body(
+def summed_body(
     layer_inputs,
     pre_acts,
     layer_outputs,
@@ -85,7 +89,242 @@
     return (inputs[None], preact[None], outputs[None], duals[None], weight[None], offset[None])
 
 
+MESH = pl.DeviceIdType.MESH
+NN = (((1,), (0,)), ((), ()))
+NT = (((1,), (1,)), ((), ()))
+
+
+def split(x):
+    high = x.astype(jnp.bfloat16)
+    return high, (x - high.astype(jnp.float32)).astype(jnp.bfloat16)
+
+
+def dot3(left, right, dims=NN):
+    def one(a, b):
+        return lax.dot_general(a, b, dims, preferred_element_type=jnp.float32)
+
+    return one(left[0], right[0]) + (one(left[0], right[1]) + one(left[1], right[0]))
+
+
+def softplus(v):
+    return jnp.maximum(v, 0.0) + jnp.log1p(jnp.exp(-jnp.abs(v)))
+
+
+def permuted(order, x):
+    rows = x.shape[0]
+    stored = lax.broadcasted_iota(jnp.int32, (rows, rows), 0)
+    pick = jnp.where(stored == order, 1.0, 0.0).T.astype(jnp.bfloat16)
+    high, rest = split(x)
+    rest = x - high.astype(jnp.float32)
+    mid, low = split(rest)
+
+    def one(part):
+        return jnp.dot(pick, part, preferred_element_type=jnp.float32)
+
+    return one(high) + (one(mid) + one(low))
+
+
+def kernel(
+    n, layers,
+    p_ref, z_ref, q_ref, u_ref, w_ref, b_ref, qb_ref, ub_ref, pb_ref, order_ref,
+    p_out, z_out, q_out, u_out, w_out, b_out,
+    p_all, z_all, coupling, p_next, own_coupling, w_hi, w_lo, p_hi, p_lo, pt_hi, pt_lo, target0, t_hi, t_lo, change,
+    z_right, z_left, z_recv, p_right, p_left, p_recv, layer_send, layer_recv,
+):
+    rows, width = p_ref.shape
+    total = rows * n
+    me, layer = lax.axis_index("dp"), lax.axis_index("layer")
+    scale = step_weight / total
+    has_left, has_right = me > 0, me < n - 1
+    has_below, has_above = layer > 0, layer < layers - 1
+
+    barrier = pltpu.get_barrier_semaphore()
+    for there, axis, index in (
+        (has_left, "dp", me - 1), (has_right, "dp", me + 1),
+        (has_below, "layer", layer - 1), (has_above, "layer", layer + 1),
+    ):
+        @pl.when(there)
+        def _():
+            pl.semaphore_signal(barrier, inc=1, device_id={axis: index}, device_id_type=MESH)
+
+    own_coupling[...] = u_ref[...] - q_ref[...]
+    w = w_ref[...]
+    w_hi[...], w_lo[...] = split(w)
+    ends = [jnp.where(there, 1, 0) for there in (has_left, has_right, has_below, has_above)]
+    pl.semaphore_wait(barrier, ends[0] + ends[1] + ends[2] + ends[3])
+
+    def z_copy(owner, to_right, own=False):
+        return pltpu.make_async_remote_copy(
+            src_ref=z_ref if own else z_all.at[owner], dst_ref=z_all.at[owner],
+            send_sem=(z_right if to_right else z_left).at[owner], recv_sem=z_recv.at[owner],
+            device_id={"dp": me + 1 if to_right else me - 1}, device_id_type=MESH,
+        )
+
+    def p_copy(owner, to_right):
+        return pltpu.make_async_remote_copy(
+            src_ref=p_all.at[owner], dst_ref=p_all.at[owner],
+            send_sem=(p_right if to_right else p_left).at[owner], recv_sem=p_recv.at[owner],
+            device_id={"dp": me + 1 if to_right else me - 1}, device_id_type=MESH,
+        )
+
+    up = pltpu.make_async_remote_copy(
+        src_ref=own_coupling, dst_ref=coupling, send_sem=layer_send.at[0], recv_sem=layer_recv.at[0],
+        device_id={"layer": layer + 1}, device_id_type=MESH,
+    )
+    down = pltpu.make_async_remote_copy(
+        src_ref=p_all.at[me], dst_ref=p_next, send_sem=layer_send.at[1], recv_sem=layer_recv.at[1],
+        device_id={"layer": layer - 1}, device_id_type=MESH,
+    )
+
+    pl.when(has_above)(lambda: up.start())
+    pl.when(has_right)(lambda: z_copy(me, True, True).start())
+    pl.when(has_left)(lambda: z_copy(me, False, True).start())
+
+    weight = (w_hi[...], w_lo[...])
+    p, z, bias = p_ref[...], z_ref[...], b_ref[...]
+    residual = dot3(split(p), weight) + bias - z
+    back = dot3(split(residual), weight, NT)
+
+    @pl.when(jnp.logical_not(has_below))
+    def _():
+        coupling[...] = permuted(order_ref[...], ub_ref[...] - qb_ref[...])
+
+    pl.when(has_below)(lambda: up.wait_recv())
+    p = p - step_input * (back + (coupling[...] + p))
+    p_all[me] = p
+    p_out[...] = p
+    pl.when(has_right)(lambda: p_copy(me, True).start())
+    pl.when(has_left)(lambda: p_copy(me, False).start())
+    pl.when(has_below)(lambda: down.start())
+
+    @pl.when(jnp.logical_not(has_above))
+    def _():
+        p_next[...] = permuted(order_ref[...], pb_ref[...])
+
+    pt_hi[pl.ds(width, 16), :] = jnp.ones((16, total), jnp.bfloat16)
+    pt_lo[pl.ds(width, 16), :] = jnp.zeros((16, total), jnp.bfloat16)
+
+    def block(owner):
+        return pl.ds(pl.multiple_of(owner * rows, rows), rows)
+
+    def take_p(owner, value, z_value=None):
+        high, low = split(value)
+        p_hi[block(owner), :], p_lo[block(owner), :] = high, low
+        across = split(value.T)
+        pt_hi[pl.ds(0, width), block(owner)] = across[0]
+        pt_lo[pl.ds(0, width), block(owner)] = across[1]
+        product = dot3((high, low), (w_hi[...], w_lo[...])) + b_ref[...]
+        target0[block(owner), :] = product if z_value is None else product - z_value
+
+    take_p(me, p, z)
+    for s in range(1, n):
+        @pl.when(me >= s)
+        def _():
+            p_copy(me - s, True).wait_recv()
+            pl.when(has_right)(lambda: p_copy(me - s, True).start())
+        @pl.when(me + s < n)
+        def _():
+            p_copy(me + s, False).wait_recv()
+            pl.when(has_left)(lambda: p_copy(me + s, False).start())
+        if s == n - 1:
+            pass
+        @pl.when(me >= s)
+        def _():
+            take_p(me - s, p_all[me - s])
+        @pl.when(me + s < n)
+        def _():
+            take_p(me + s, p_all[me + s])
+
+    def z_arrives(s, use):
+        @pl.when(me >= s)
+        def _():
+            z_copy(me - s, True).wait_recv()
+            pl.when(has_right)(lambda: z_copy(me - s, True).start())
+        @pl.when(me + s < n)
+        def _():
+            z_copy(me + s, False).wait_recv()
+            pl.when(has_left)(lambda: z_copy(me + s, False).start())
+        pl.when(me >= s)(lambda: use(me - s))
+        pl.when(me + s < n)(lambda: use(me + s))
+
+    def subtract(owner):
+        target0[block(owner), :] -= z_all[owner]
+
+    z_arrives(1, subtract)
+
+    stacked = (p_hi[...], p_lo[...])
+    moment = scale * (dot3(stacked, stacked, NT) + 1.0)
+    moment_parts = split(moment)
+    same = lax.broadcasted_iota(jnp.int32, (total, total), 0) == lax.broadcasted_iota(jnp.int32, (total, total), 1)
+    steps = jnp.where(same, 3.0, 0.0) - 3.0 * moment + dot3(moment_parts, moment_parts)
+    t = scale * dot3((pt_hi[...], pt_lo[...]), split(steps))
+    t_hi[...], t_lo[...] = split(t)
+    change[...] = dot3((t_hi[...], t_lo[...]), split(target0[...]))
+
+    def add(owner):
+        change[...] -= dot3((t_hi[:, block(owner)], t_lo[:, block(owner)]), split(z_all[owner]))
+
+    for s in range(2, n):
+        z_arrives(s, add)
+
+    w = w_ref[...] - change[pl.ds(0, width), :]
+    bias = b_ref[...] - change[pl.ds(width, 1), :]
+    w_out[...] = w
+    b_out[...] = bias
+    target = dot3(split(p_all[me]), split(w)) + bias
+    z, q, u = z_ref[...], q_ref[...], u_ref[...]
+    z = z - step_preact * ((z - target) + (softplus(z) - q) * jax.nn.sigmoid(z))
+    z_out[...] = z
+    pl.when(has_above)(lambda: down.wait_recv())
+    after = p_next[...]
+    q = (penalty_nu * softplus(z) + u + penalty_rho * after) / (penalty_nu + penalty_rho)
+    q_out[...] = q
+    u_out[...] = u + penalty_rho * (after - q)
+
+    for owner in range(n):
+        @pl.when(jnp.logical_and(me >= owner, has_right))
+        def _():
+            z_copy(owner, True).wait_send()
+            p_copy(owner, True).wait_send()
+        @pl.when(jnp.logical_and(me <= owner, has_left))
+        def _():
+            z_copy(owner, False).wait_send()
+            p_copy(owner, False).wait_send()
+    pl.when(has_above)(lambda: up.wait_send())
+    pl.when(has_below)(lambda: down.wait_send())
+
+
+def gathered_body(n, layers, layer_inputs, pre_acts, layer_outputs, multipliers, weights, biases, prev_outputs, prev_multipliers, next_inputs, row_order):
+    rows, width = prev_outputs.shape
+    total = rows * n
+    f32, b16 = jnp.float32, jnp.bfloat16
+    dma = pltpu.SemaphoreType.DMA
+    vmem = pl.BlockSpec(memory_space=pltpu.VMEM)
+    block = jax.ShapeDtypeStruct((rows, width), f32)
+    outs = pl.pallas_call(
+        functools.partial(kernel, n, layers),
+        out_shape=(block,) * 4 + (jax.ShapeDtypeStruct((width, width), f32), jax.ShapeDtypeStruct((1, width), f32)),
+        in_specs=[vmem] * 10,
+        out_specs=(vmem,) * 6,
+        scratch_shapes=[
+            pltpu.VMEM((n, rows, width), f32), pltpu.VMEM((n, rows, width), f32),
+            pltpu.VMEM((rows, width), f32), pltpu.VMEM((rows, width), f32), pltpu.VMEM((rows, width), f32),
+            pltpu.VMEM((width, width), b16), pltpu.VMEM((width, width), b16),
+            pltpu.VMEM((total, width), b16), pltpu.VMEM((total, width), b16),
+            pltpu.VMEM((width + 16, total), b16), pltpu.VMEM((width + 16, total), b16),
+            pltpu.VMEM((total, width), f32),
+            pltpu.VMEM((width + 16, total), b16), pltpu.VMEM((width + 16, total), b16),
+            pltpu.VMEM((width + 16, width), f32),
+            dma((n,)), dma((n,)), dma((n,)), dma((n,)), dma((n,)), dma((n,)), dma((2,)), dma((2,)),
+        ],
+        compiler_params=pltpu.CompilerParams(collective_id=0, has_side_effects=True, vmem_limit_bytes=48 * 2**20),
+    )(layer_inputs[0], pre_acts[0], layer_outputs[0], multipliers[0], weights[0], biases, prev_outputs, prev_multipliers, next_inputs, row_order)
+    return tuple(x[None] for x in outs[:5]) + (outs[5],)
+
+
 def solution(mesh):
+    n, layers = mesh.shape["dp"], mesh.shape["layer"]
+    body = functools.partial(gathered_body, n, layers) if n <= 8 else summed_body
     return jax.shard_map(
         body,
         mesh=mesh,

time: 131 us -> 58.7 us (0.45)
  waiting for transfers between devices: 73.5 us -> 0 us
  Pallas kernels: 0 us -> 44.8 us
  matrix products: 16.1 us -> 0 us
  between operations: 14.3 us -> 0.67 us
  blocking collectives: 12.6 us -> 0 us
  starting transfers between devices: 8.38 us -> 0 us
  local copies, waits for them, and re-layouts: 5.07 us -> 12.9 us
    psum x1 -> x0, waiting for transfers between devices: 73.5 us -> none  [body(): lax.psum((matmul(inputs.T, inputs), matmul(inputs.T, preact), jnp.sum(inp...]
    pallas_call x0 -> x1, Pallas kernels: none -> 44.8 us  [gathered_body(): pl.pallas_call(functools.partial(kernel, n, layers), out_shape=(block,) *...]
    dot_general x11 -> x0, matrix products: 16.1 us -> none  [matmul(): return jnp.dot(left, right, precision=lax.Precision.HIGHEST)]
    psum x1 -> x0, blocking collectives: 12.6 us -> none  [body(): lax.psum((matmul(inputs.T, inputs), matmul(inputs.T, preact), jnp.sum(inp...]
    unnamed x32 -> x26, local copies, waits for them, and re-layouts: 2.81 us -> 12.9 us
    ppermute x3 -> x0, starting transfers between devices: 8.34 us -> none  [from_behind(): return lax.ppermute(x, axis, pairs)]
    gather x3 -> x0, local copies, waits for them, and re-layouts: 2.26 us -> none  [the longest x1 0.76 us: body(): edge_duals = jnp.take(prev_multipliers, row_perm, axis=0)]
  transfers between devices with their start and end apart: 4 -> 0, of which waited for: 1 -> 0; matrix products, arithmetic and copies ran while one was open for 10% -> 0% of each run, Pallas kernels for 0% -> 0%
where the time goes in v1:
time: 58.7 us; the launch traced here: 58.3 us
  Pallas kernels  44.8 us (76%)
  local copies, waits for them, and re-layouts  12.9 us (22%)
  between operations  0.67 us (1%)
    pallas_call x1, Pallas kernels, gathered_body(): pl.pallas_call(functools.partial(kernel, n, layers), out_shape=(block,) *...  44.8 us
    unnamed x26, local copies, waits for them, and re-layouts  12.9 us

profile of v1, /device:TPU:0, one launch (start us, length us, event | category | flops | bytes accessed | tf_op | source)
XLA Modules:
  0.0 58.3 jit_solution(12856146060997891605)
XLA Ops:
  0.6 0.0 copy-start.8
  0.6 0.0 copy-start.9
  0.7 0.7 %copy-done.8 = f32[1,512]{1,0:T(1,128)S(1)} copy-done((f32[1,512]{1,0:T(1,128)S(1)}, f32[1,512]{1,0:T(1,128)}, u32[]{:S(2)}) %copy-start.8) | copy-done | bytes 2072
  1.3 0.0 copy-done.9
  1.3 0.0 copy-start
  1.3 1.2 %copy-done = f32[1,512,512]{2,1,0:T(8,128)S(1)} copy-done((f32[1,512,512]{2,1,0:T(8,128)S(1)}, f32[1,512,512]{2,1,0:T(8,128)}, u32[]{:S(2)}) %copy-start) | copy-done | bytes 1048600
  2.5 0.0 copy-start.1
  2.5 0.9 %copy-done.1 = f32[1,128,512]{2,1,0:T(8,128)S(1)} copy-done((f32[1,128,512]{2,1,0:T(8,128)S(1)}, f32[1,128,512]{2,1,0:T(8,128)}, u32[]{:S(2)}) %copy-start.1) | copy-done | bytes 262168
  3.5 0.0 copy-start.2
  3.5 0.9 %copy-done.2 = f32[1,128,512]{2,1,0:T(8,128)S(1)} copy-done((f32[1,128,512]{2,1,0:T(8,128)S(1)}, f32[1,128,512]{2,1,0:T(8,128)}, u32[]{:S(2)}) %copy-start.2) | copy-done | bytes 262168
  4.4 0.0 copy-start.3
  4.5 0.9 %copy-done.3 = f32[1,128,512]{2,1,0:T(8,128)S(1)} copy-done((f32[1,128,512]{2,1,0:T(8,128)S(1)}, f32[1,128,512]{2,1,0:T(8,128)}, u32[]{:S(2)}) %copy-start.3) | copy-done | bytes 262168
  5.4 0.0 copy-start.4
  5.4 0.9 %copy-done.4 = f32[1,128,512]{2,1,0:T(8,128)S(1)} copy-done((f32[1,128,512]{2,1,0:T(8,128)S(1)}, f32[1,128,512]{2,1,0:T(8,128)}, u32[]{:S(2)}) %copy-start.4) | copy-done | bytes 262168
  6.3 0.0 copy-start.5
  6.4 0.9 %copy-done.5 = f32[128,512]{1,0:T(8,128)S(1)} copy-done((f32[128,512]{1,0:T(8,128)S(1)}, f32[128,512]{1,0:T(8,128)}, u32[]{:S(2)}) %copy-start.5) | copy-done | bytes 262168
  7.3 0.0 copy-start.6
  7.3 0.9 %copy-done.6 = f32[128,512]{1,0:T(8,128)S(1)} copy-done((f32[128,512]{1,0:T(8,128)S(1)}, f32[128,512]{1,0:T(8,128)}, u32[]{:S(2)}) %copy-start.6) | copy-done | bytes 262168
  8.2 0.0 copy-start.7
  8.3 0.9 %copy-done.7 = f32[128,512]{1,0:T(8,128)S(1)} copy-done((f32[128,512]{1,0:T(8,128)S(1)}, f32[128,512]{1,0:T(8,128)}, u32[]{:S(2)}) %copy-start.7) | copy-done | bytes 262168
  9.2 44.8 %shard_map.145 = (f32[128,512]{1,0:T(8,128)S(1)}, f32[128,512]{1,0:T(8,128)S(1)}, f32[128,512]{1,0:T(8,128)S(1)}, f32[128,512]{1,0:T(8,128)S(1)}, f32[512,512]{1,0:T(8,128)S(1)}, /*index=5*/f32[1,512]{1,0:T(1,128)S(1)}) custom-call(f32[128,512]{1,0:T(8,128)S(1)} %bitcast.16, f32[128,512]{1,0:T(8,128)S(1)} %bitcast.17, f32[128,512]{1,0:T(8,128)S(1)} %bitcast.18, ...), custom_call_target="tpu_custom_call" | custom-call | tf_op jit(solution)/shard_map/pallas_call | solution.py:304
  54.0 0.7 %copy.22 = f32[1,128,512]{2,1,0:T(8,128)} copy(f32[1,128,512]{2,1,0:T(8,128)S(1)} %bitcast.15) | data formatting | bytes 524288
  54.7 0.7 %copy.23 = f32[1,128,512]{2,1,0:T(8,128)} copy(f32[1,128,512]{2,1,0:T(8,128)S(1)} %bitcast.14) | data formatting | bytes 524288
  55.4 0.7 %copy.24 = f32[1,128,512]{2,1,0:T(8,128)} copy(f32[1,128,512]{2,1,0:T(8,128)S(1)} %bitcast.13) | data formatting | bytes 524288
  56.1 0.7 %copy.25 = f32[1,128,512]{2,1,0:T(8,128)} copy(f32[1,128,512]{2,1,0:T(8,128)S(1)} %bitcast.12) | data formatting | bytes 524288
  56.8 1.0 %copy.26 = f32[1,512,512]{2,1,0:T(8,128)} copy(f32[1,512,512]{2,1,0:T(8,128)S(1)} %bitcast.10) | data formatting | bytes 2097152
  57.8 0.6 copy.27
Async XLA Ops:
  0.6 0.7 %copy-start.8 = (f32[1,512]{1,0:T(1,128)S(1)}, f32[1,512]{1,0:T(1,128)}, u32[]{:S(2)}) copy-start(f32[1,512]{1,0:T(1,128)} %b_ref.1) | copy-start | bytes 6148
  0.6 0.7 %copy-start.9 = (s32[1,128]{1,0:T(1,128)S(1)}, s32[1,128]{1,0:T(1,128)}, u32[]{:S(2)}) copy-start(s32[1,128]{1,0:T(1,128)} %order_ref.1) | copy-start | bytes 1540
  1.3 1.2 %copy-start = (f32[1,512,512]{2,1,0:T(8,128)S(1)}, f32[1,512,512]{2,1,0:T(8,128)}, u32[]{:S(2)}) copy-start(f32[1,512,512]{2,1,0:T(8,128)} %param.14) | copy-start | bytes 3145732
  2.5 0.9 %copy-start.1 = (f32[1,128,512]{2,1,0:T(8,128)S(1)}, f32[1,128,512]{2,1,0:T(8,128)}, u32[]{:S(2)}) copy-start(f32[1,128,512]{2,1,0:T(8,128)} %param.10) | copy-start | bytes 786436
  3.5 0.9 %copy-start.2 = (f32[1,128,512]{2,1,0:T(8,128)S(1)}, f32[1,128,512]{2,1,0:T(8,128)}, u32[]{:S(2)}) copy-start(f32[1,128,512]{2,1,0:T(8,128)} %param.11) | copy-start | bytes 786436
  4.4 0.9 %copy-start.3 = (f32[1,128,512]{2,1,0:T(8,128)S(1)}, f32[1,128,512]{2,1,0:T(8,128)}, u32[]{:S(2)}) copy-start(f32[1,128,512]{2,1,0:T(8,128)} %param.12) | copy-start | bytes 786436
  5.4 0.9 %copy-start.4 = (f32[1,128,512]{2,1,0:T(8,128)S(1)}, f32[1,128,512]{2,1,0:T(8,128)}, u32[]{:S(2)}) copy-start(f32[1,128,512]{2,1,0:T(8,128)} %param.13) | copy-start | bytes 786436
  6.3 0.9 %copy-start.5 = (f32[128,512]{1,0:T(8,128)S(1)}, f32[128,512]{1,0:T(8,128)}, u32[]{:S(2)}) copy-start(f32[128,512]{1,0:T(8,128)} %qb_ref.1) | copy-start | bytes 786436
  7.3 0.9 %copy-start.6 = (f32[128,512]{1,0:T(8,128)S(1)}, f32[128,512]{1,0:T(8,128)}, u32[]{:S(2)}) copy-start(f32[128,512]{1,0:T(8,128)} %ub_ref.1) | copy-start | bytes 786436
  8.2 0.9 %copy-start.7 = (f32[128,512]{1,0:T(8,128)S(1)}, f32[128,512]{1,0:T(8,128)}, u32[]{:S(2)}) copy-start(f32[128,512]{1,0:T(8,128)} %pb_ref.1) | copy-start | bytes 786436

commit v2 on v1

--- a/solution.py
+++ b/solution.py
@@ -126,10 +126,11 @@
 
 def kernel(
     n, layers,
+    p_hbm, z_hbm, q_hbm, u_hbm, w_hbm, b_hbm, qb_hbm, ub_hbm, pb_hbm, order_hbm,
+    p_out, z_out, q_out, u_out, w_out, b_out,
     p_ref, z_ref, q_ref, u_ref, w_ref, b_ref, qb_ref, ub_ref, pb_ref, order_ref,
-    p_out, z_out, q_out, u_out, w_out, b_out,
     p_all, z_all, coupling, p_next, own_coupling, w_hi, w_lo, p_hi, p_lo, pt_hi, pt_lo, target0, t_hi, t_lo, change,
-    z_right, z_left, z_recv, p_right, p_left, p_recv, layer_send, layer_recv,
+    z_right, z_left, z_recv, p_right, p_left, p_recv, layer_send, layer_recv, loads, stores, z_new,
 ):
     rows, width = p_ref.shape
     total = rows * n
@@ -147,9 +148,18 @@
         def _():
             pl.semaphore_signal(barrier, inc=1, device_id={axis: index}, device_id_type=MESH)
 
+    load = {}
+    for i, (name, source, target) in enumerate((
+        ("u", u_hbm, u_ref), ("q", q_hbm, q_ref), ("z", z_hbm, z_ref), ("w", w_hbm, w_ref), ("p", p_hbm, p_ref),
+        ("b", b_hbm, b_ref), ("order", order_hbm, order_ref), ("ub", ub_hbm, ub_ref), ("qb", qb_hbm, qb_ref),
+        ("pb", pb_hbm, pb_ref),
+    )):
+        load[name] = pltpu.make_async_copy(source, target, loads.at[i])
+        load[name].start()
+    load["u"].wait()
+    load["q"].wait()
     own_coupling[...] = u_ref[...] - q_ref[...]
-    w = w_ref[...]
-    w_hi[...], w_lo[...] = split(w)
+    load["z"].wait()
     ends = [jnp.where(there, 1, 0) for there in (has_left, has_right, has_below, has_above)]
     pl.semaphore_wait(barrier, ends[0] + ends[1] + ends[2] + ends[3])
 
@@ -180,6 +190,9 @@
     pl.when(has_right)(lambda: z_copy(me, True, True).start())
     pl.when(has_left)(lambda: z_copy(me, False, True).start())
 
+    for name in ("w", "p", "b", "order", "ub", "qb", "pb"):
+        load[name].wait()
+    w_hi[...], w_lo[...] = split(w_ref[...])
     weight = (w_hi[...], w_lo[...])
     p, z, bias = p_ref[...], z_ref[...], b_ref[...]
     residual = dot3(split(p), weight) + bias - z
@@ -192,7 +205,12 @@
     pl.when(has_below)(lambda: up.wait_recv())
     p = p - step_input * (back + (coupling[...] + p))
     p_all[me] = p
-    p_out[...] = p
+    store = {}
+    for i, (name, source, target) in enumerate((
+        ("p", p_all.at[me], p_out), ("w", w_ref, w_out), ("b", b_ref, b_out), ("z", z_new, z_out), ("q", q_ref, q_out), ("u", u_ref, u_out),
+    )):
+        store[name] = pltpu.make_async_copy(source, target, stores.at[i])
+    store["p"].start()
     pl.when(has_right)(lambda: p_copy(me, True).start())
     pl.when(has_left)(lambda: p_copy(me, False).start())
     pl.when(has_below)(lambda: down.start())
@@ -269,17 +287,22 @@
 
     w = w_ref[...] - change[pl.ds(0, width), :]
     bias = b_ref[...] - change[pl.ds(width, 1), :]
-    w_out[...] = w
-    b_out[...] = bias
+    w_ref[...] = w
+    b_ref[...] = bias
+    store["w"].start()
+    store["b"].start()
     target = dot3(split(p_all[me]), split(w)) + bias
     z, q, u = z_ref[...], q_ref[...], u_ref[...]
     z = z - step_preact * ((z - target) + (softplus(z) - q) * jax.nn.sigmoid(z))
-    z_out[...] = z
+    z_new[...] = z
+    store["z"].start()
     pl.when(has_above)(lambda: down.wait_recv())
     after = p_next[...]
     q = (penalty_nu * softplus(z) + u + penalty_rho * after) / (penalty_nu + penalty_rho)
-    q_out[...] = q
-    u_out[...] = u + penalty_rho * (after - q)
+    q_ref[...] = q
+    store["q"].start()
+    u_ref[...] = u + penalty_rho * (after - q)
+    store["u"].start()
 
     for owner in range(n):
         @pl.when(jnp.logical_and(me >= owner, has_right))
@@ -292,6 +315,21 @@
             p_copy(owner, False).wait_send()
     pl.when(has_above)(lambda: up.wait_send())
     pl.when(has_below)(lambda: down.wait_send())
+    for copy in store.values():
+        copy.wait()
+
+
+def store_kernel(*refs):
+    sources, targets, held, sems = refs[:6], refs[6:12], refs[12:18], refs[18]
+    ins = [pltpu.make_async_copy(a, b, sems.at[0, i]) for i, (a, b) in enumerate(zip(sources, held))]
+    outs = [pltpu.make_async_copy(a, b, sems.at[1, i]) for i, (a, b) in enumerate(zip(held, targets))]
+    for copy in ins:
+        copy.start()
+    for taken, copy in zip(ins, outs):
+        taken.wait()
+        copy.start()
+    for copy in outs:
+        copy.wait()
 
 
 def gathered_body(n, layers, layer_inputs, pre_acts, layer_outputs, multipliers, weights, biases, prev_outputs, prev_multipliers, next_inputs, row_order):
@@ -299,14 +337,19 @@
     total = rows * n
     f32, b16 = jnp.float32, jnp.bfloat16
     dma = pltpu.SemaphoreType.DMA
-    vmem = pl.BlockSpec(memory_space=pltpu.VMEM)
     block = jax.ShapeDtypeStruct((rows, width), f32)
+    hbm = pl.BlockSpec(memory_space=pltpu.HBM)
+    shapes = (block,) * 4 + (jax.ShapeDtypeStruct((width, width), f32), jax.ShapeDtypeStruct((1, width), f32))
     outs = pl.pallas_call(
         functools.partial(kernel, n, layers),
-        out_shape=(block,) * 4 + (jax.ShapeDtypeStruct((width, width), f32), jax.ShapeDtypeStruct((1, width), f32)),
-        in_specs=[vmem] * 10,
-        out_specs=(vmem,) * 6,
+        out_shape=shapes,
+        in_specs=[hbm] * 10,
+        out_specs=(hbm,) * 6,
         scratch_shapes=[
+            *(pltpu.VMEM((rows, width), f32),) * 4,
+            pltpu.VMEM((width, width), f32), pltpu.VMEM((1, width), f32),
+            *(pltpu.VMEM((rows, width), f32),) * 3,
+            pltpu.VMEM((1, rows), jnp.int32),
             pltpu.VMEM((n, rows, width), f32), pltpu.VMEM((n, rows, width), f32),
             pltpu.VMEM((rows, width), f32), pltpu.VMEM((rows, width), f32), pltpu.VMEM((rows, width), f32),
             pltpu.VMEM((width, width), b16), pltpu.VMEM((width, width), b16),
@@ -315,10 +358,14 @@
             pltpu.VMEM((total, width), f32),
             pltpu.VMEM((width + 16, total), b16), pltpu.VMEM((width + 16, total), b16),
             pltpu.VMEM((width + 16, width), f32),
-            dma((n,)), dma((n,)), dma((n,)), dma((n,)), dma((n,)), dma((n,)), dma((2,)), dma((2,)),
+            dma((n,)), dma((n,)), dma((n,)), dma((n,)), dma((n,)), dma((n,)), dma((2,)), dma((2,)), dma((10,)), dma((6,)), pltpu.VMEM((rows, width), f32),
         ],
-        compiler_params=pltpu.CompilerParams(collective_id=0, has_side_effects=True, vmem_limit_bytes=48 * 2**20),
+        compiler_params=pltpu.CompilerParams(collective_id=0, has_side_effects=True),
     )(layer_inputs[0], pre_acts[0], layer_outputs[0], multipliers[0], weights[0], biases, prev_outputs, prev_multipliers, next_inputs, row_order)
+    outs = pl.pallas_call(
+        store_kernel, out_shape=shapes, in_specs=[hbm] * 6, out_specs=(hbm,) * 6,
+        scratch_shapes=[*(pltpu.VMEM(x.shape, x.dtype) for x in shapes), dma((2, 6))],
+    )(*outs)
     return tuple(x[None] for x in outs[:5]) + (outs[5],)
 
 

time: 58.7 us -> 49.4 us (0.84)
  local copies, waits for them, and re-layouts: 12.9 us -> 0 us
  Pallas kernels: 44.8 us -> 48.6 us
    unnamed x26 -> x0, local copies, waits for them, and re-layouts: 12.9 us -> none
    pallas_call x1 -> x2, Pallas kernels: 44.8 us -> 48.6 us  [the longest x1 45.9 us: gathered_body(): pl.pallas_call(functools.partial(kernel, n, layers), out_shape=shapes, in...]
where the time goes in v2:
time: 49.4 us; the launch traced here: 49.2 us
  Pallas kernels  48.6 us (98%)
  between operations  0.64 us (1%)
    pallas_call x1, Pallas kernels, gathered_body(): pl.pallas_call(functools.partial(kernel, n, layers), out_shape=shapes, in...  45.9 us
    pallas_call x1, Pallas kernels, gathered_body(): pl.pallas_call(store_kernel, out_shape=shapes, in_specs=[hbm] * 6, out_sp...  2.63 us

profile of v2, /device:TPU:0, one launch (start us, length us, event | category | flops | bytes accessed | tf_op | source)
XLA Modules:
  0.0 49.2 jit_solution(11265637078242832309)
XLA Ops:
  0.6 45.9 %shard_map.145 = (f32[128,512]{1,0:T(8,128)}, f32[128,512]{1,0:T(8,128)}, f32[128,512]{1,0:T(8,128)}, f32[128,512]{1,0:T(8,128)}, f32[512,512]{1,0:T(8,128)}, /*index=5*/f32[1,512]{1,0:T(1,128)}) custom-call(f32[128,512]{1,0:T(8,128)} %bitcast.11, f32[128,512]{1,0:T(8,128)} %bitcast.12, f32[128,512]{1,0:T(8,128)} %bitcast.13, f32[128,512]{1,0:T(8,128)} %bitcast.14, ...), custom_call_target="tpu_custom_call" | custom-call | tf_op jit(solution)/shard_map/pallas_call | solution.py:343
  46.6 2.6 %shard_map.146 = (f32[128,512]{1,0:T(8,128)}, f32[128,512]{1,0:T(8,128)}, f32[128,512]{1,0:T(8,128)}, f32[128,512]{1,0:T(8,128)}, f32[512,512]{1,0:T(8,128)}, /*index=5*/f32[1,512]{1,0:T(1,128)}) custom-call(f32[128,512]{1,0:T(8,128)} %get-tuple-element.18.refs_0_, f32[128,512]{1,0:T(8,128)} %get-tuple-element.19.refs_1_, ...), custom_call_target="tpu_custom_call" | custom-call | tf_op jit(solution)/shard_map/pallas_call | solution.py:365

commit v3 on v2

--- a/solution.py
+++ b/solution.py
@@ -150,15 +150,12 @@
 
     load = {}
     for i, (name, source, target) in enumerate((
-        ("u", u_hbm, u_ref), ("q", q_hbm, q_ref), ("z", z_hbm, z_ref), ("w", w_hbm, w_ref), ("p", p_hbm, p_ref),
+        ("z", z_hbm, z_ref), ("u", u_hbm, u_ref), ("q", q_hbm, q_ref), ("w", w_hbm, w_ref), ("p", p_hbm, p_ref),
         ("b", b_hbm, b_ref), ("order", order_hbm, order_ref), ("ub", ub_hbm, ub_ref), ("qb", qb_hbm, qb_ref),
         ("pb", pb_hbm, pb_ref),
     )):
         load[name] = pltpu.make_async_copy(source, target, loads.at[i])
         load[name].start()
-    load["u"].wait()
-    load["q"].wait()
-    own_coupling[...] = u_ref[...] - q_ref[...]
     load["z"].wait()
     ends = [jnp.where(there, 1, 0) for there in (has_left, has_right, has_below, has_above)]
     pl.semaphore_wait(barrier, ends[0] + ends[1] + ends[2] + ends[3])
@@ -186,9 +183,12 @@
         device_id={"layer": layer - 1}, device_id_type=MESH,
     )
 
-    pl.when(has_above)(lambda: up.start())
     pl.when(has_right)(lambda: z_copy(me, True, True).start())
     pl.when(has_left)(lambda: z_copy(me, False, True).start())
+    load["u"].wait()
+    load["q"].wait()
+    own_coupling[...] = u_ref[...] - q_ref[...]
+    pl.when(has_above)(lambda: up.start())
 
     for name in ("w", "p", "b", "order", "ub", "qb", "pb"):
         load[name].wait()
@@ -234,41 +234,27 @@
         product = dot3((high, low), (w_hi[...], w_lo[...])) + b_ref[...]
         target0[block(owner), :] = product if z_value is None else product - z_value
 
+    def relay(s, copy):
+        @pl.when(me >= s)
+        def _():
+            copy(me - s, True).wait_recv()
+            pl.when(has_right)(lambda: copy(me - s, True).start())
+
+        @pl.when(me + s < n)
+        def _():
+            copy(me + s, False).wait_recv()
+            pl.when(has_left)(lambda: copy(me + s, False).start())
+
+    def use(s, step):
+        pl.when(me >= s)(lambda: step(me - s))
+        pl.when(me + s < n)(lambda: step(me + s))
+
     take_p(me, p, z)
     for s in range(1, n):
-        @pl.when(me >= s)
-        def _():
-            p_copy(me - s, True).wait_recv()
-            pl.when(has_right)(lambda: p_copy(me - s, True).start())
-        @pl.when(me + s < n)
-        def _():
-            p_copy(me + s, False).wait_recv()
-            pl.when(has_left)(lambda: p_copy(me + s, False).start())
-        if s == n - 1:
-            pass
-        @pl.when(me >= s)
-        def _():
-            take_p(me - s, p_all[me - s])
-        @pl.when(me + s < n)
-        def _():
-            take_p(me + s, p_all[me + s])
-
-    def z_arrives(s, use):
-        @pl.when(me >= s)
-        def _():
-            z_copy(me - s, True).wait_recv()
-            pl.when(has_right)(lambda: z_copy(me - s, True).start())
-        @pl.when(me + s < n)
-        def _():
-            z_copy(me + s, False).wait_recv()
-            pl.when(has_left)(lambda: z_copy(me + s, False).start())
-        pl.when(me >= s)(lambda: use(me - s))
-        pl.when(me + s < n)(lambda: use(me + s))
-
-    def subtract(owner):
-        target0[block(owner), :] -= z_all[owner]
-
-    z_arrives(1, subtract)
+        relay(s, p_copy)
+        if s < n - 1:
+            relay(s, z_copy)
+        use(s, lambda owner: take_p(owner, p_all[owner], z_all[owner] if s < n - 1 else None))
 
     stacked = (p_hi[...], p_lo[...])
     moment = scale * (dot3(stacked, stacked, NT) + 1.0)
@@ -282,8 +268,9 @@
     def add(owner):
         change[...] -= dot3((t_hi[:, block(owner)], t_lo[:, block(owner)]), split(z_all[owner]))
 
-    for s in range(2, n):
-        z_arrives(s, add)
+    if n > 1:
+        relay(n - 1, z_copy)
+        use(n - 1, add)
 
     w = w_ref[...] - change[pl.ds(0, width), :]
     bias = b_ref[...] - change[pl.ds(width, 1), :]

time: 49.4 us -> 47.2 us (0.955)
  Pallas kernels: 48.6 us -> 46.4 us
    pallas_call x1, Pallas kernels: 45.9 us -> 43.7 us  [gathered_body(): pl.pallas_call(functools.partial(kernel, n, layers), out_shape=shapes, in...]
where the time goes in v3:
time: 47.2 us; the launch traced here: 47 us
  Pallas kernels  46.4 us (98%)
  between operations  0.64 us (1%)
    pallas_call x1, Pallas kernels, gathered_body(): pl.pallas_call(functools.partial(kernel, n, layers), out_shape=shapes, in...  43.7 us
    pallas_call x1, Pallas kernels, gathered_body(): pl.pallas_call(store_kernel, out_shape=shapes, in_specs=[hbm] * 6, out_sp...  2.63 us

profile of v3, /device:TPU:0, one launch (start us, length us, event | category | flops | bytes accessed | tf_op | source)
XLA Modules:
  0.0 47.0 jit_solution(8570244826385793513)
XLA Ops:
  0.6 43.7 %shard_map.145 = (f32[128,512]{1,0:T(8,128)}, f32[128,512]{1,0:T(8,128)}, f32[128,512]{1,0:T(8,128)}, f32[128,512]{1,0:T(8,128)}, f32[512,512]{1,0:T(8,128)}, /*index=5*/f32[1,512]{1,0:T(1,128)}) custom-call(f32[128,512]{1,0:T(8,128)} %bitcast.11, f32[128,512]{1,0:T(8,128)} %bitcast.12, f32[128,512]{1,0:T(8,128)} %bitcast.13, f32[128,512]{1,0:T(8,128)} %bitcast.14, ...), custom_call_target="tpu_custom_call" | custom-call | tf_op jit(solution)/shard_map/pallas_call | solution.py:330
  44.4 2.6 %shard_map.146 = (f32[128,512]{1,0:T(8,128)}, f32[128,512]{1,0:T(8,128)}, f32[128,512]{1,0:T(8,128)}, f32[128,512]{1,0:T(8,128)}, f32[512,512]{1,0:T(8,128)}, /*index=5*/f32[1,512]{1,0:T(1,128)}) custom-call(f32[128,512]{1,0:T(8,128)} %get-tuple-element.18.refs_0_, f32[128,512]{1,0:T(8,128)} %get-tuple-element.19.refs_1_, ...), custom_call_target="tpu_custom_call" | custom-call | tf_op jit(solution)/shard_map/pallas_call | solution.py:352

commit v4 on v3

--- a/solution.py
+++ b/solution.py
@@ -90,6 +90,7 @@
 
 
 MESH = pl.DeviceIdType.MESH
+VMEM_BYTES = 67043328
 NN = (((1,), (0,)), ((), ()))
 NT = (((1,), (1,)), ((), ()))
 
@@ -130,7 +131,7 @@
     p_out, z_out, q_out, u_out, w_out, b_out,
     p_ref, z_ref, q_ref, u_ref, w_ref, b_ref, qb_ref, ub_ref, pb_ref, order_ref,
     p_all, z_all, coupling, p_next, own_coupling, w_hi, w_lo, p_hi, p_lo, pt_hi, pt_lo, target0, t_hi, t_lo, change,
-    z_right, z_left, z_recv, p_right, p_left, p_recv, layer_send, layer_recv, loads, stores, z_new,
+    z_right, z_left, z_recv, p_right, p_left, p_recv, layer_send, layer_recv, loads,
 ):
     rows, width = p_ref.shape
     total = rows * n
@@ -205,12 +206,7 @@
     pl.when(has_below)(lambda: up.wait_recv())
     p = p - step_input * (back + (coupling[...] + p))
     p_all[me] = p
-    store = {}
-    for i, (name, source, target) in enumerate((
-        ("p", p_all.at[me], p_out), ("w", w_ref, w_out), ("b", b_ref, b_out), ("z", z_new, z_out), ("q", q_ref, q_out), ("u", u_ref, u_out),
-    )):
-        store[name] = pltpu.make_async_copy(source, target, stores.at[i])
-    store["p"].start()
+    p_out[...] = p
     pl.when(has_right)(lambda: p_copy(me, True).start())
     pl.when(has_left)(lambda: p_copy(me, False).start())
     pl.when(has_below)(lambda: down.start())
@@ -274,22 +270,17 @@
 
     w = w_ref[...] - change[pl.ds(0, width), :]
     bias = b_ref[...] - change[pl.ds(width, 1), :]
-    w_ref[...] = w
-    b_ref[...] = bias
-    store["w"].start()
-    store["b"].start()
+    w_out[...] = w
+    b_out[...] = bias
     target = dot3(split(p_all[me]), split(w)) + bias
     z, q, u = z_ref[...], q_ref[...], u_ref[...]
     z = z - step_preact * ((z - target) + (softplus(z) - q) * jax.nn.sigmoid(z))
-    z_new[...] = z
-    store["z"].start()
+    z_out[...] = z
     pl.when(has_above)(lambda: down.wait_recv())
     after = p_next[...]
     q = (penalty_nu * softplus(z) + u + penalty_rho * after) / (penalty_nu + penalty_rho)
-    q_ref[...] = q
-    store["q"].start()
-    u_ref[...] = u + penalty_rho * (after - q)
-    store["u"].start()
+    q_out[...] = q
+    u_out[...] = u + penalty_rho * (after - q)
 
     for owner in range(n):
         @pl.when(jnp.logical_and(me >= owner, has_right))
@@ -302,20 +293,14 @@
             p_copy(owner, False).wait_send()
     pl.when(has_above)(lambda: up.wait_send())
     pl.when(has_below)(lambda: down.wait_send())
-    for copy in store.values():
-        copy.wait()
 
 
 def store_kernel(*refs):
-    sources, targets, held, sems = refs[:6], refs[6:12], refs[12:18], refs[18]
-    ins = [pltpu.make_async_copy(a, b, sems.at[0, i]) for i, (a, b) in enumerate(zip(sources, held))]
-    outs = [pltpu.make_async_copy(a, b, sems.at[1, i]) for i, (a, b) in enumerate(zip(held, targets))]
-    for copy in ins:
+    sources, targets, sems = refs[:6], refs[6:12], refs[12]
+    copies = [pltpu.make_async_copy(a, b, sems.at[i]) for i, (a, b) in enumerate(zip(sources, targets))]
+    for copy in copies:
         copy.start()
-    for taken, copy in zip(ins, outs):
-        taken.wait()
-        copy.start()
-    for copy in outs:
+    for copy in copies:
         copy.wait()
 
 
@@ -327,11 +312,13 @@
     block = jax.ShapeDtypeStruct((rows, width), f32)
     hbm = pl.BlockSpec(memory_space=pltpu.HBM)
     shapes = (block,) * 4 + (jax.ShapeDtypeStruct((width, width), f32), jax.ShapeDtypeStruct((1, width), f32))
+    vm = pl.BlockSpec(memory_space=pltpu.VMEM)
+    kept = (sum(x.size for x in shapes) * 4 + 2**14) // 2**12 * 2**12
     outs = pl.pallas_call(
         functools.partial(kernel, n, layers),
-        out_shape=shapes,
+        out_shape=tuple(pltpu.VMEM(x.shape, x.dtype) for x in shapes),
         in_specs=[hbm] * 10,
-        out_specs=(hbm,) * 6,
+        out_specs=(vm,) * 6,
         scratch_shapes=[
             *(pltpu.VMEM((rows, width), f32),) * 4,
             pltpu.VMEM((width, width), f32), pltpu.VMEM((1, width), f32),
@@ -345,13 +332,13 @@
             pltpu.VMEM((total, width), f32),
             pltpu.VMEM((width + 16, total), b16), pltpu.VMEM((width + 16, total), b16),
             pltpu.VMEM((width + 16, width), f32),
-            dma((n,)), dma((n,)), dma((n,)), dma((n,)), dma((n,)), dma((n,)), dma((2,)), dma((2,)), dma((10,)), dma((6,)), pltpu.VMEM((rows, width), f32),
+            dma((n,)), dma((n,)), dma((n,)), dma((n,)), dma((n,)), dma((n,)), dma((2,)), dma((2,)), dma((10,)),
         ],
-        compiler_params=pltpu.CompilerParams(collective_id=0, has_side_effects=True),
+        compiler_params=pltpu.CompilerParams(collective_id=0, has_side_effects=True, vmem_limit_bytes=VMEM_BYTES - kept),
     )(layer_inputs[0], pre_acts[0], layer_outputs[0], multipliers[0], weights[0], biases, prev_outputs, prev_multipliers, next_inputs, row_order)
     outs = pl.pallas_call(
-        store_kernel, out_shape=shapes, in_specs=[hbm] * 6, out_specs=(hbm,) * 6,
-        scratch_shapes=[*(pltpu.VMEM(x.shape, x.dtype) for x in shapes), dma((2, 6))],
+        store_kernel, out_shape=shapes, in_specs=[vm] * 6, out_specs=(hbm,) * 6,
+        scratch_shapes=[dma((6,))], compiler_params=pltpu.CompilerParams(vmem_limit_bytes=2**20),
     )(*outs)
     return tuple(x[None] for x in outs[:5]) + (outs[5],)
 

time: 47.2 us -> 45.1 us (0.956)
  Pallas kernels: 46.4 us -> 44.3 us
    pallas_call x2, Pallas kernels: 46.4 us -> 44.3 us  [the longest x1 42.9 us: gathered_body(): pl.pallas_call(functools.partial(kernel, n, layers), out_shape=tuple((plt...]
where the time goes in v4:
time: 45.1 us; the launch traced here: 44.9 us
  Pallas kernels  44.3 us (98%)
  between operations  0.64 us (1%)
    pallas_call x1, Pallas kernels, gathered_body(): pl.pallas_call(functools.partial(kernel, n, layers), out_shape=tuple((plt...  42.9 us
    pallas_call x1, Pallas kernels, gathered_body(): pl.pallas_call(store_kernel, out_shape=shapes, in_specs=[vm] * 6, out_spe...  1.37 us

profile of v4, /device:TPU:0, one launch (start us, length us, event | category | flops | bytes accessed | tf_op | source)
XLA Modules:
  0.0 44.9 jit_solution(11862829573206621367)
XLA Ops:
  0.6 42.9 %shard_map.145 = (f32[128,512]{1,0:T(8,128)S(1)}, f32[128,512]{1,0:T(8,128)S(1)}, f32[128,512]{1,0:T(8,128)S(1)}, f32[128,512]{1,0:T(8,128)S(1)}, f32[512,512]{1,0:T(8,128)S(1)}, /*index=5*/f32[1,512]{1,0:T(1,128)S(1)}) custom-call(f32[128,512]{1,0:T(8,128)} %bitcast.11, f32[128,512]{1,0:T(8,128)} %bitcast.12, f32[128,512]{1,0:T(8,128)} %bitcast.13, ...), custom_call_target="tpu_custom_call" | custom-call | tf_op jit(solution)/shard_map/pallas_call | solution.py:317
  43.5 1.4 %shard_map.146 = (f32[128,512]{1,0:T(8,128)}, f32[128,512]{1,0:T(8,128)}, f32[128,512]{1,0:T(8,128)}, f32[128,512]{1,0:T(8,128)}, f32[512,512]{1,0:T(8,128)}, /*index=5*/f32[1,512]{1,0:T(1,128)}) custom-call(f32[128,512]{1,0:T(8,128)S(1)} %get-tuple-element.18.refs_0_, f32[128,512]{1,0:T(8,128)S(1)} %get-tuple-element.19.refs_1_, ...), custom_call_target="tpu_custom_call" | custom-call | tf_op jit(solution)/shard_map/pallas_call | solution.py:339

commit v5 on v4

--- a/solution.py
+++ b/solution.py
@@ -131,7 +131,7 @@
     p_out, z_out, q_out, u_out, w_out, b_out,
     p_ref, z_ref, q_ref, u_ref, w_ref, b_ref, qb_ref, ub_ref, pb_ref, order_ref,
     p_all, z_all, coupling, p_next, own_coupling, w_hi, w_lo, p_hi, p_lo, pt_hi, pt_lo, target0, t_hi, t_lo, change,
-    z_right, z_left, z_recv, p_right, p_left, p_recv, layer_send, layer_recv, loads,
+    z_right, z_left, z_recv, p_right, p_left, p_recv, layer_send, layer_recv, loads, products,
 ):
     rows, width = p_ref.shape
     total = rows * n
@@ -221,9 +221,15 @@
     def block(owner):
         return pl.ds(pl.multiple_of(owner * rows, rows), rows)
 
+    p_hi[...] = jnp.zeros((total, width), jnp.bfloat16)
+    p_lo[...] = jnp.zeros((total, width), jnp.bfloat16)
+
     def take_p(owner, value, z_value=None):
         high, low = split(value)
         p_hi[block(owner), :], p_lo[block(owner), :] = high, low
+        stacked = (p_hi[...], p_lo[...])
+        products[block(owner), :] = dot3((high, low), stacked, NT)
+        products[:, block(owner)] = dot3(stacked, (high, low), NT)
         across = split(value.T)
         pt_hi[pl.ds(0, width), block(owner)] = across[0]
         pt_lo[pl.ds(0, width), block(owner)] = across[1]
@@ -252,8 +258,7 @@
             relay(s, z_copy)
         use(s, lambda owner: take_p(owner, p_all[owner], z_all[owner] if s < n - 1 else None))
 
-    stacked = (p_hi[...], p_lo[...])
-    moment = scale * (dot3(stacked, stacked, NT) + 1.0)
+    moment = scale * (products[...] + 1.0)
     moment_parts = split(moment)
     same = lax.broadcasted_iota(jnp.int32, (total, total), 0) == lax.broadcasted_iota(jnp.int32, (total, total), 1)
     steps = jnp.where(same, 3.0, 0.0) - 3.0 * moment + dot3(moment_parts, moment_parts)
@@ -332,7 +337,7 @@
             pltpu.VMEM((total, width), f32),
             pltpu.VMEM((width + 16, total), b16), pltpu.VMEM((width + 16, total), b16),
             pltpu.VMEM((width + 16, width), f32),
-            dma((n,)), dma((n,)), dma((n,)), dma((n,)), dma((n,)), dma((n,)), dma((2,)), dma((2,)), dma((10,)),
+            dma((n,)), dma((n,)), dma((n,)), dma((n,)), dma((n,)), dma((n,)), dma((2,)), dma((2,)), dma((10,)), pltpu.VMEM((total, total), f32),
         ],
         compiler_params=pltpu.CompilerParams(collective_id=0, has_side_effects=True, vmem_limit_bytes=VMEM_BYTES - kept),
     )(layer_inputs[0], pre_acts[0], layer_outputs[0], multipliers[0], weights[0], biases, prev_outputs, prev_multipliers, next_inputs, row_order)

time: 45.1 us -> 45.1 us (level)
  no operation moved by 1% of the time
where the time goes in v5:
time: 45.1 us; the launch traced here: 44.9 us
  Pallas kernels  44.3 us (98%)
  between operations  0.64 us (1%)
    pallas_call x1, Pallas kernels, gathered_body(): pl.pallas_call(functools.partial(kernel, n, layers), out_shape=tuple((plt...  42.9 us
    pallas_call x1, Pallas kernels, gathered_body(): pl.pallas_call(store_kernel, out_shape=shapes, in_specs=[vm] * 6, out_spe...  1.37 us

profile of v5, /device:TPU:0, one launch (start us, length us, event | category | flops | bytes accessed | tf_op | source)
XLA Modules:
  0.0 44.9 jit_solution(9412684327165630553)
XLA Ops:
  0.6 42.9 %shard_map.145 = (f32[128,512]{1,0:T(8,128)S(1)}, f32[128,512]{1,0:T(8,128)S(1)}, f32[128,512]{1,0:T(8,128)S(1)}, f32[128,512]{1,0:T(8,128)S(1)}, f32[512,512]{1,0:T(8,128)S(1)}, /*index=5*/f32[1,512]{1,0:T(1,128)S(1)}) custom-call(f32[128,512]{1,0:T(8,128)} %bitcast.11, f32[128,512]{1,0:T(8,128)} %bitcast.12, f32[128,512]{1,0:T(8,128)} %bitcast.13, ...), custom_call_target="tpu_custom_call" | custom-call | tf_op jit(solution)/shard_map/pallas_call | solution.py:322
  43.5 1.4 %shard_map.146 = (f32[128,512]{1,0:T(8,128)}, f32[128,512]{1,0:T(8,128)}, f32[128,512]{1,0:T(8,128)}, f32[128,512]{1,0:T(8,128)}, f32[512,512]{1,0:T(8,128)}, /*index=5*/f32[1,512]{1,0:T(1,128)}) custom-call(f32[128,512]{1,0:T(8,128)S(1)} %get-tuple-element.18.refs_0_, f32[128,512]{1,0:T(8,128)S(1)} %get-tuple-element.19.refs_1_, ...), custom_call_target="tpu_custom_call" | custom-call | tf_op jit(solution)/shard_map/pallas_call | solution.py:344
